TPU v7x, 256 devices: a whole 4x4x8 slice. The times are simulated.
256 devices in a mesh: ia: 8 (over y_lo, x), ja: 4 (over y_hi, core), ka: 8 (over z).
Axes of the slice: x: 4, y: 4 (y_hi: 2, y_lo: 2; y = y_hi * 2 + y_lo), z: 8, core: 2. Of those that a mesh axis runs over, the one named last changes fastest.
Arguments:
- tensor: bfloat16 [2048, 512, 1024], P('ia', 'ja', 'ka'), may hold values from 0 to 122880
- matrix: bfloat16 [2048, 262144], P(None, ('ia', 'ja', 'ka')), may hold values from 0 to 1024000
- first_factor: bfloat16 [2048, 256], P('ia'), may hold values from 0.05 to 2
- second_factor: bfloat16 [512, 256], P('ja'), may hold values from 0.05 to 2
- time_factor: bfloat16 [1024, 256], P('ka'), may hold values from 0.05 to 2
- column_factor: bfloat16 [262144, 256], P(('ia', 'ja', 'ka')), may hold values from 0.05 to 2
Outputs:
- first_new: bfloat16 [2048, 256], P('ia')
- second_new: bfloat16 [512, 256], P('ja')
- time_new: bfloat16 [1024, 256], P('ka')
All inputs are finite; a program needn't handle non-finite values.
Results may differ from a plain program's by a relative error of at most 0.00075.
The roundings to bfloat16 on the way count: a program that leaves them out, or rounds other values in their place, can miss the bound.
Values may be sent and summed in bfloat16 or wider, within the bound.
A program may use at most 128 MiB of HBM per device.

v0:
```python
import jax
import jax.numpy as jnp
from jax import lax
from jax.sharding import PartitionSpec as P


def cross_product(values):
    return jnp.dot(values.T, values, preferred_element_type=jnp.float32)


def rescale(factor, numerator, gram_total):
    widened = factor.astype(jnp.float32)
    denominator = jnp.dot(widened, gram_total, precision=lax.Precision.HIGHEST)
    return (widened * numerator / denominator).astype(jnp.bfloat16)


def on_device(tensor, matrix, first_factor, second_factor, time_factor, column_factor):
    first_rows = lax.axis_index("ia") == 0
    first_plane = lax.axis_index("ja") == 0
    first_time = lax.axis_index("ka") == 0
    gram_second = jnp.where(first_rows & first_time, cross_product(second_factor), 0.0)
    gram_time = jnp.where(first_rows & first_plane, cross_product(time_factor), 0.0)
    gram_column = cross_product(column_factor)
    gram_second, gram_time, gram_column = lax.psum(
        (gram_second, gram_time, gram_column), ("ia", "ja", "ka")
    )
    gram_total = gram_second * gram_time + gram_column
    tile_i, tile_j, tile_k = tensor.shape
    rank_size = first_factor.shape[1]
    khatri = (
        (
            second_factor.astype(jnp.float32)[:, None, :]
            * time_factor.astype(jnp.float32)[None, :, :]
        )
        .astype(jnp.bfloat16)
        .reshape(tile_j * tile_k, rank_size)
    )
    slab = jnp.dot(
        tensor.reshape(tile_i, tile_j * tile_k), khatri, preferred_element_type=jnp.float32
    )
    coupled = jnp.dot(matrix, column_factor, preferred_element_type=jnp.float32)
    offset = lax.axis_index("ia") * tile_i
    coupled = lax.psum(coupled, ("ia", "ja", "ka"))
    slab = lax.psum(slab, ("ja", "ka"))
    numerator = slab + lax.dynamic_slice_in_dim(coupled, offset, tile_i, 0)
    first_new = rescale(first_factor, numerator, gram_total)
    weighted = lax.dot_general(
        tensor, first_new, (((0,), (0,)), ((), ())), preferred_element_type=jnp.float32
    )
    plane_sum = jnp.sum(weighted * time_factor.astype(jnp.float32)[None, :, :], axis=1)
    gram_first = jnp.where(first_time, cross_product(first_new), 0.0)
    plane_sum, gram_first = lax.psum((plane_sum, gram_first), ("ia", "ka"))
    second_new = rescale(second_factor, plane_sum, gram_first * gram_time)
    time_sum = jnp.sum(weighted * second_new.astype(jnp.float32)[:, None, :], axis=0)
    gram_new = jnp.where(first_rows, cross_product(second_new), 0.0)
    time_sum, gram_new = lax.psum((time_sum, gram_new), ("ia", "ja"))
    time_new = rescale(time_factor, time_sum, gram_first * gram_new)
    return (first_new, second_new, time_new)


def solution(mesh):
    return jax.shard_map(
        on_device,
        mesh=mesh,
        in_specs=(
            P("ia", "ja", "ka"),
            P(None, ("ia", "ja", "ka")),
            P("ia", None),
            P("ja", None),
            P("ka", None),
            P(("ia", "ja", "ka"), None),
        ),
        out_specs=(P("ia", None), P("ja", None), P("ka", None)),
        check_vma=False,
    )
```

profile of v0, /device:TPU:1, one launch (start us, length us, event | category | flops | bytes accessed | tf_op | source)
XLA Modules:
  0.0 1287.7 jit_solution(12729258825692898810)
XLA Ops:
  7.2 1.0 copy.26
  8.2 0.1 copy.27
  8.4 13.1 %copy.32 = bf16[256,128,128]{0,2,1:T(8,128)(2,1)} copy(bf16[256,128,128]{2,1,0:T(8,128)(2,1)} %param.6) | data formatting | bytes 16777216 | tf_op args[0]
  21.7 6.4 fusion.4
  28.3 0.9 convolution_select_fusion.3
  29.2 4.8 fusion.14
  34.0 0.9 convolution_select_fusion.2
  34.9 1.0 fusion.15
  36.1 257.2 %all-reduce.8.cloned.1.call-done = f32[256,256]{0,1:T(8,128)} async-done(((f32[256,256]{0,1:T(8,128)}), f32[256,256]{0,1:T(8,128)}) %all-reduce.8.cloned.1.call-update) | async-done | bytes 262160 | tf_op jit(solution)/shard_map/psum | solution.py:44
  293.3 272.6 %all-reduce.10.cloned.1.call-done = (f32[256,256]{1,0:T(8,128)}, f32[256,256]{1,0:T(8,128)}, f32[256,256]{1,0:T(8,128)}, f32[2048,256]{0,1:T(8,128)}) async-done(((f32[256,256]{1,0:T(8,128)}, f32[256,256]{1,0:T(8,128)}, f32[256,256]{1,0:T(8,128)}, f32[2048,256]{0,1:T(8,128)}), (f32[256,256]{1,0:T(8,128)}, f32[256,256]{1,0:T(8,128)}, f32[256,256]{1,0:T(8,128)}, ...) | async-done | bytes 2883600 | tf_op jit(solution)/shard_map/psum | solution.py:24
  565.9 1.7 fusion.5
  567.6 0.9 convolution_select_fusion.1
  568.5 11.5 multiply_reduce_fusion.1
  580.0 0.8 copy.33
  580.9 540.1 %all-reduce.12.cloned.1.call-done = (f32[256,256]{1,0:T(8,128)}, f32[128,256]{0,1:T(8,128)}) async-done(((f32[256,256]{1,0:T(8,128)}, f32[128,256]{0,1:T(8,128)}), (f32[256,256]{1,0:T(8,128)}, f32[128,256]{0,1:T(8,128)})) %all-reduce.12.cloned.1.call-update) | async-done | bytes 393232 | tf_op jit(solution)/shard_map/psum | solution.py:52
  1120.9 1.4 fusion.9
  1122.4 0.9 convolution_select_fusion
  1123.3 7.7 multiply_reduce_fusion
  1131.0 0.8 copy.35
  1131.8 0.8 copy.36
  1132.5 0.7 copy.37
  1133.3 145.7 %all-reduce.14.cloned.1.call-done = (f32[256,256]{1,0:T(8,128)}, f32[128,256]{0,1:T(8,128)}) async-done(((f32[256,256]{1,0:T(8,128)}, f32[128,256]{0,1:T(8,128)}), (f32[256,256]{1,0:T(8,128)}, f32[128,256]{0,1:T(8,128)})) %all-reduce.14.cloned.1.call-update) | async-done | bytes 393232 | tf_op jit(solution)/shard_map/psum | solution.py:56
  1279.0 1.4 fusion.8
  1280.4 0.7 copy.38
  (24 shorter events, 0.7 us)
Async XLA Ops:
  7.2 22.0 %copy-start = (bf16[1024,256]{1,0:T(8,128)(2,1)S(1)}, bf16[1024,256]{1,0:T(8,128)(2,1)}, u32[]{:S(2)}) copy-start(bf16[1024,256]{1,0:T(8,128)(2,1)} %param.11) | copy-start | bytes 1572868
  7.2 286.2 %all-reduce.8.cloned.1.call-start = ((), (), s32[]{:S(2)}) async-start(), calls=%async_computation | async-start | bytes 524288 | tf_op jit(solution)/shard_map/psum | solution.py:44
  8.3 13.1 %copy-start.3 = (bf16[128,256]{1,0:T(8,128)(2,1)S(1)}, bf16[128,256]{1,0:T(8,128)(2,1)}, u32[]{:S(2)}) copy-start(bf16[128,256]{1,0:T(8,128)(2,1)} %param.9) | copy-start | bytes 196612
  28.2 5.8 copy-start.4
  28.2 537.7 %all-reduce.10.cloned.1.call-start = ((), (), s32[]{:S(2)}) async-start(), calls=%async_computation.1 | async-start | bytes 5767168 | tf_op jit(solution)/shard_map/psum | solution.py:24
  29.2 6.9 copy-start.5
  36.0 1084.9 %all-reduce.12.cloned.1.call-start = ((), (), s32[]{:S(2)}) async-start(), calls=%async_computation.2 | async-start | bytes 786432 | tf_op jit(solution)/shard_map/psum | solution.py:52
  568.5 552.4 %copy-start.1 = (f32[256,256]{1,0:T(8,128)S(1)}, f32[256,256]{1,0:T(8,128)}, u32[]{:S(2)}) copy-start(f32[256,256]{1,0:T(8,128)} %get-tuple-element.11) | copy-start | bytes 786436
  580.8 698.2 %all-reduce.14.cloned.1.call-start = ((), (), s32[]{:S(2)}) async-start(), calls=%async_computation.3 | async-start | bytes 786432 | tf_op jit(solution)/shard_map/psum | solution.py:56
  1123.3 155.7 %copy-start.2 = (f32[256,256]{1,0:T(8,128)S(1)}, f32[256,256]{1,0:T(8,128)}, u32[]{:S(2)}) copy-start(f32[256,256]{1,0:T(8,128)} %get-tuple-element.13) | copy-start | bytes 786436
Sparse Core Ops, SparseCore 0:
  28.3 264.9 all-reduce.7
  300.3 265.5 all-reduce.9
  580.9 539.9 all-reduce.11
  1131.9 147.0 all-reduce.13
where the time goes:
time: 1290 us
  waiting for transfers between devices  1220 us (95%)
  matrix products  31.9 us (2%)
  local copies, waits for them, and re-layouts  18.4 us (1%)
  between operations  13.9 us (1%)
    psum x1, waiting for transfers between devices, on_device(): plane_sum, gram_first = lax.psum((plane_sum, gram_first), ('ia', 'ka'))  540 us
    psum x1, waiting for transfers between devices, on_device(): lax.psum((gram_second, gram_time, gram_column), ('ia', 'ja', 'ka'))  273 us
    psum x1, waiting for transfers between devices, on_device(): slab = lax.psum(slab, ('ja', 'ka'))  257 us
    psum x1, waiting for transfers between devices, on_device(): time_sum, gram_new = lax.psum((time_sum, gram_new), ('ia', 'ja'))  146 us
  transfers between devices with their start and end apart: 4, of which 4 were waited for; matrix products, arithmetic and copies ran while one was open for 1% of the time, Pallas kernels for 0%

commit v1 on v0

v1 whole, which is shorter than its diff:
```python
import functools

import jax
import jax.numpy as jnp
from jax import lax
from jax.experimental import pallas as pl
from jax.experimental.pallas import tpu as pltpu
from jax.sharding import PartitionSpec as P

F32 = jnp.float32
BF16 = jnp.bfloat16


def dot(a, b):
    return jnp.dot(a, b, preferred_element_type=F32)


def dot_nt(a, b):
    return lax.dot_general(a, b, (((1,), (1,)), ((), ())), preferred_element_type=F32)


def identity(n):
    rows = lax.broadcasted_iota(jnp.int32, (n, n), 0)
    columns = lax.broadcasted_iota(jnp.int32, (n, n), 1)
    return (rows == columns).astype(F32).astype(BF16)


def transposed(values):
    return dot_nt(identity(values.shape[1]), values)


def exact_product(gram, factor):
    rows = gram.shape[0]
    high = gram.astype(BF16).astype(F32)
    rest = gram - high
    middle = rest.astype(BF16).astype(F32)
    low = (rest - middle).astype(BF16).astype(F32)
    parts = [high, middle, low]
    while (rows * len(parts)) % 16:
        parts.append(jnp.zeros_like(high))
    stacked = dot_nt(jnp.concatenate(parts, axis=0).astype(BF16), factor)
    return stacked[:rows] + (stacked[rows : 2 * rows] + stacked[2 * rows : 3 * rows])


def kernel(
    sizes,
    tensor_ref,
    matrix_ref,
    first_ref,
    second_ref,
    time_ref,
    column_ref,
    first_out,
    second_out,
    time_out,
    tens,
    perm,
    wide,
    mats,
    col_t,
    coup,
    pair_in,
    ring_in,
    slab_acc,
    slab_half,
    slab_in,
    sum_half,
    sum_in,
    gc_loc,
    gc_in,
    gs_loc,
    gs_in,
    gt_loc,
    gt_in,
    gt_sum,
    ga_in,
    first_t,
    second_t,
    time_t,
    second_f,
    time_f,
    fn_in,
    fn_rows,
    gf_loc,
    gfa_in,
    gfb_in,
    plane,
    ps_loc,
    ps_in,
    pa_in,
    sn_in,
    sn_groups,
    gn_loc,
    gn_in,
    tsum,
    ts_loc,
    ts_in,
    tn_in,
    mat_sem,
    tens_sem,
    pair_send,
    pair_recv,
    send_sem,
    recv_sem,
):
    nia, nja, nka, rank, ti, tj, tk = sizes
    nyh = nja // 2
    slots = nja * nka
    q1, q2, q3 = rank // slots, rank // nka, rank // (nia * nja)
    groups = nka * nyh
    half = tj // 2
    ia, ja, ka = lax.axis_index("ia"), lax.axis_index("ja"), lax.axis_index("ka")
    core = lax.rem(ja, 2)
    other = 1 - core
    yh = ja // 2
    slot1 = ka * nja + ja
    group = ka * nyh + yh
    slot3 = ia * nja + ja

    def wrap(value, n):
        return lax.rem(value + n, n)

    def remote(src, dst, s_sem, r_sem, dia, dja, dka):
        return pltpu.make_async_remote_copy(
            src_ref=src,
            dst_ref=dst,
            send_sem=s_sem,
            recv_sem=r_sem,
            device_id=(dia, dja, dka),
            device_id_type=pl.DeviceIdType.MESH,
        )

    def wait_bytes(ref, sem):
        pltpu.make_async_copy(ref, ref, sem).wait()

    def block_of(s):
        return wrap(ia + 1 + s, nia)

    def mat_copy(s):
        rows = pl.ds(pl.multiple_of(block_of(s) * ti, ti), ti)
        return pltpu.make_async_copy(matrix_ref.at[rows, :], mats.at[s], mat_sem.at[s])

    def tens_copy(b):
        rows = pl.ds(b * 16, 16)
        return pltpu.make_async_copy(tensor_ref.at[rows], tens.at[rows], tens_sem.at[b])

    @pl.loop(0, nia)
    def _(s):
        mat_copy(s).start()

    @pl.loop(0, ti // 16)
    def _(b):
        tens_copy(b).start()

    barrier = pltpu.get_barrier_semaphore()

    @pl.loop(1, slots)
    def _(t):
        pl.semaphore_signal(
            barrier,
            inc=1,
            device_id=(ia, wrap(ja + lax.rem(t, nja), nja), wrap(ka + t // nja, nka)),
            device_id_type=pl.DeviceIdType.MESH,
        )

    @pl.loop(nja, nia * nja)
    def _(t):
        pl.semaphore_signal(
            barrier,
            inc=1,
            device_id=(wrap(ia + t // nja, nia), wrap(ja + lax.rem(t, nja), nja), ka),
            device_id_type=pl.DeviceIdType.MESH,
        )

    col_t[...] = transposed(column_ref[...]).astype(BF16)
    pl.semaphore_wait(barrier, slots - 1 + (nia - 1) * nja)

    def pair_copy(s):
        return remote(
            coup.at[s, other], pair_in.at[s], pair_send.at[s], pair_recv.at[s], ia, ja + 1 - 2 * core, ka
        )

    def coupled_block(s):
        mat_copy(s).wait()
        block = dot_nt(col_t[...], mats[s]).reshape(groups, 2, q1, ti)
        coup[s, 0] = block[:, 0]
        coup[s, 1] = block[:, 1]
        pair_copy(s).start()

    def paired_sum(s):
        pair_copy(s).wait_recv()
        coup[s, core] = coup[s, core] + pair_in[s]

    def ring_copy(s):
        return remote(
            coup.at[s, core], ring_in.at[s], send_sem.at[0], recv_sem.at[0], block_of(s), ja, ka
        )

    coupled_block(0)

    @pl.loop(1, nia)
    def _(s):
        coupled_block(s)
        paired_sum(s - 1)
        ring_copy(s - 1).start()

    gc_loc[...] = dot(col_t[...], column_ref[...]).reshape(slots, q1, rank)
    time_tr = transposed(time_ref[...])
    time_t[...] = time_tr.reshape(nia * nja, q3, tk)
    gt_loc[...] = dot(time_tr.astype(BF16), time_ref[...]).reshape(nka, q2, rank)
    second_tr = transposed(second_ref[...])
    second_t[...] = second_tr.reshape(nka, q2, tj)
    gs_loc[...] = dot(second_tr.astype(BF16), second_ref[...]).reshape(slots, q1, rank)
    first_t[...] = transposed(first_ref[...]).reshape(slots, q1, ti)
    second_f[...] = second_ref[...].astype(F32)
    time_f[...] = time_ref[...].astype(F32)
    gc_in[slot1] = gc_loc[slot1]
    gs_in[ja] = gs_loc[slot1]
    gt_in[ka] = gt_loc[ka]

    @pl.loop(1, slots)
    def _(t):
        dja, dka = wrap(ja + lax.rem(t, nja), nja), wrap(ka + t // nja, nka)
        remote(
            gc_loc.at[dka * nja + dja], gc_in.at[slot1], send_sem.at[1], recv_sem.at[1], ia, dja, dka
        ).start()

    @pl.loop(1, nja)
    def _(t):
        dja = wrap(ja + t, nja)
        remote(
            gs_loc.at[ka * nja + dja], gs_in.at[ja], send_sem.at[2], recv_sem.at[2], ia, dja, ka
        ).start()

    @pl.loop(1, nka)
    def _(t):
        dka = wrap(ka + t, nka)
        remote(gt_loc.at[dka], gt_in.at[ka], send_sem.at[3], recv_sem.at[3], ia, ja, dka).start()

    paired_sum(nia - 1)

    rows = lax.broadcasted_iota(jnp.int32, (256, 256), 0)
    columns = lax.broadcasted_iota(jnp.int32, (256, 256), 1)
    order = (lax.rem(rows, 16) == columns // 16) & (rows // 16 == lax.rem(columns, 16))
    order = order.astype(F32).astype(BF16)

    @pl.loop(0, ti // 16)
    def _(b):
        tens_copy(b).wait()
        i0 = pl.multiple_of(b * 16, 16)
        for c in range(half // 16):
            low = tens[pl.ds(i0, 16), 16 * c : 16 * c + 16, :].reshape(256, tk)
            high = tens[pl.ds(i0, 16), half + 16 * c : half + 16 * c + 16, :].reshape(256, tk)
            block = dot(order, jnp.concatenate([low, high], axis=1))
            perm[16 * c : 16 * c + 16, pl.ds(i0, 16), :] = block.astype(BF16).reshape(16, 16, 2 * tk)

    slab_acc[...] = jnp.zeros_like(slab_acc)

    @pl.loop(0, half // 4)
    def _(b):
        total = slab_acc[...]
        for u in range(4):
            j = b * 4 + u
            khatri = jnp.concatenate(
                [time_f[...] * second_f[pl.ds(j, 1), :], time_f[...] * second_f[pl.ds(j + half, 1), :]],
                axis=0,
            ).astype(BF16)
            total = total + dot(perm[j], khatri)
        slab_acc[...] = total

    slab_tr = slab_acc[...].T.reshape(groups, 2, q1, ti)
    slab_half[0] = slab_tr[:, 0]
    slab_half[1] = slab_tr[:, 1]
    slab_copy = remote(
        slab_half.at[other], slab_in, send_sem.at[4], recv_sem.at[4], ia, ja + 1 - 2 * core, ka
    )
    slab_copy.start()

    wait_bytes(gc_in.at[pl.ds(0, slots - 1)], recv_sem.at[1])
    ga_in[ia] = jnp.sum(gc_in[...], axis=0)

    @pl.loop(1, nia)
    def _(t):
        remote(
            ga_in.at[ia], ga_in.at[ia], send_sem.at[5], recv_sem.at[5], wrap(ia + t, nia), ja, ka
        ).start()

    wait_bytes(gs_in.at[pl.ds(0, nja - 1)], recv_sem.at[2])
    wait_bytes(gt_in.at[pl.ds(0, nka - 1)], recv_sem.at[3])
    gt_sum[...] = jnp.sum(gt_in[...], axis=0).reshape(nja, q1, rank)
    gram_part = jnp.sum(gs_in[...], axis=0) * gt_sum[ja]

    wait_bytes(ring_in, recv_sem.at[0])
    slab_copy.wait_recv()
    sum_half[...] = (
        coup[nia - 1, core] + jnp.sum(ring_in[...], axis=0) + (slab_half[core] + slab_in[...])
    )
    sum_in[group] = sum_half[group]

    @pl.loop(1, groups)
    def _(t):
        dyh, dka = wrap(yh + lax.rem(t, nyh), nyh), wrap(ka + t // nyh, nka)
        remote(
            sum_half.at[dka * nyh + dyh],
            sum_in.at[group],
            send_sem.at[6],
            recv_sem.at[6],
            ia,
            2 * dyh + core,
            dka,
        ).start()

    wait_bytes(ga_in.at[pl.ds(0, nia - 1)], recv_sem.at[5])
    gram_total = gram_part + jnp.sum(ga_in[...], axis=0)
    denominator = exact_product(gram_total, first_ref[...])
    wait_bytes(sum_in.at[pl.ds(0, groups - 1)], recv_sem.at[6])
    numerator = jnp.sum(sum_in[...], axis=0)
    fn_in[slot1] = (first_t[slot1] * numerator / denominator).astype(BF16)

    @pl.loop(1, slots)
    def _(t):
        dja, dka = wrap(ja + lax.rem(t, nja), nja), wrap(ka + t // nja, nka)
        remote(
            fn_in.at[slot1], fn_in.at[slot1], send_sem.at[7], recv_sem.at[7], ia, dja, dka
        ).start()

    wait_bytes(fn_in.at[pl.ds(0, slots - 1)], recv_sem.at[7])
    fn_t = fn_in[...].astype(F32).reshape(rank, ti).astype(BF16)
    fn_rows[...] = transposed(fn_t)
    fn = fn_rows[...].astype(BF16)
    first_out[...] = fn
    gf_loc[...] = dot(fn_t, fn).reshape(nia * nja, q3, rank)
    ratio = q2 // q3
    mine = pl.ds(ka * ratio, ratio)
    gfa_in[ia] = gf_loc[mine]
    gfb_in[ia] = gf_loc[slot3]

    @pl.loop(1, nia)
    def _(t):
        dia = wrap(ia + t, nia)
        remote(gf_loc.at[mine], gfa_in.at[ia], send_sem.at[8], recv_sem.at[8], dia, ja, ka).start()
        remote(
            gf_loc.at[dia * nja + ja], gfb_in.at[ia], send_sem.at[9], recv_sem.at[9], dia, ja, ka
        ).start()

    plane[...] = jnp.zeros_like(plane)

    @pl.loop(0, ti // 8)
    def _(b):
        i0 = pl.multiple_of(b * 8, 8)
        block = dot(tens[pl.ds(i0, 8)].reshape(8 * tj, tk), time_ref[...]).reshape(8, tj, rank)
        scaled = fn_rows[pl.ds(i0, 8), :]
        total = plane[...]
        for u in range(8):
            total = total + block[u] * scaled[u : u + 1, :]
        plane[...] = total

    ps_loc[...] = plane[...].T.reshape(nka, q2, tj)
    ps_in[ka] = ps_loc[ka]

    @pl.loop(1, nka)
    def _(t):
        dka = wrap(ka + t, nka)
        remote(ps_loc.at[dka], ps_in.at[ka], send_sem.at[10], recv_sem.at[10], ia, ja, dka).start()

    def weigh(start, stop):
        @pl.loop(start, stop)
        def _(j):
            wide[j] = dot(fn_in[...].astype(F32).reshape(rank, ti).astype(BF16), perm[j])

    weigh(0, half // 2)
    wait_bytes(ps_in.at[pl.ds(0, nka - 1)], recv_sem.at[10])
    pa_in[ia] = jnp.sum(ps_in[...], axis=0)

    @pl.loop(1, nia)
    def _(t):
        remote(
            pa_in.at[ia], pa_in.at[ia], send_sem.at[11], recv_sem.at[11], wrap(ia + t, nia), ja, ka
        ).start()

    wait_bytes(gfa_in.at[pl.ds(0, nia - 1)], recv_sem.at[8])
    gram_rows = jnp.sum(gfa_in[...], axis=0).reshape(q2, rank) * gt_sum[...].reshape(q2, rank)
    second_den = exact_product(gram_rows, second_ref[...])
    weigh(half // 2, half)
    wait_bytes(pa_in.at[pl.ds(0, nia - 1)], recv_sem.at[11])
    second_num = jnp.sum(pa_in[...], axis=0)
    sn_in[ka] = (second_t[ka] * second_num / second_den).astype(BF16)

    @pl.loop(1, nka)
    def _(t):
        remote(
            sn_in.at[ka], sn_in.at[ka], send_sem.at[12], recv_sem.at[12], ia, ja, wrap(ka + t, nka)
        ).start()

    wait_bytes(sn_in.at[pl.ds(0, nka - 1)], recv_sem.at[12])
    sn_t = sn_in[...].reshape(rank, tj)
    sn_groups[...] = sn_t.reshape(nia, nja * q3, tj)
    gn_loc[...] = dot_nt(sn_groups[ia], sn_t).reshape(nja, q3, rank)
    gn_in[ja] = gn_loc[ja]

    @pl.loop(1, nja)
    def _(t):
        dja = wrap(ja + t, nja)
        remote(gn_loc.at[dja], gn_in.at[ja], send_sem.at[13], recv_sem.at[13], ia, dja, ka).start()

    tsum[...] = jnp.zeros_like(tsum)
    lane = lax.broadcasted_iota(jnp.int32, (tj, 2 * tk), 1) // tk
    row = lax.broadcasted_iota(jnp.int32, (tj, 2 * tk), 0)
    place = row - lane * half

    @pl.loop(0, half // 4)
    def _(b):
        total = tsum[...]
        for u in range(4):
            j = b * 4 + u
            pick = (place == j).astype(F32).astype(BF16)
            total = total + dot(sn_t, pick) * wide[j]
        tsum[...] = total

    ts_loc[...] = (tsum[:, :tk] + tsum[:, tk:]).reshape(nia * nja, q3, tk)
    ts_in[slot3] = ts_loc[slot3]

    @pl.loop(1, nia * nja)
    def _(t):
        dia, dja = wrap(ia + t // nja, nia), wrap(ja + lax.rem(t, nja), nja)
        remote(
            ts_loc.at[dia * nja + dja], ts_in.at[slot3], send_sem.at[14], recv_sem.at[14], dia, dja, ka
        ).start()

    second_out[...] = transposed(sn_t).astype(BF16)
    wait_bytes(gfb_in.at[pl.ds(0, nia - 1)], recv_sem.at[9])
    wait_bytes(gn_in.at[pl.ds(0, nja - 1)], recv_sem.at[13])
    gram_rows = jnp.sum(gfb_in[...], axis=0) * jnp.sum(gn_in[...], axis=0)
    time_den = exact_product(gram_rows, time_ref[...])
    wait_bytes(ts_in.at[pl.ds(0, nia * nja - 1)], recv_sem.at[14])
    time_num = jnp.sum(ts_in[...], axis=0)
    tn_in[slot3] = (time_t[slot3] * time_num / time_den).astype(BF16)

    @pl.loop(1, nia * nja)
    def _(t):
        dia, dja = wrap(ia + t // nja, nia), wrap(ja + lax.rem(t, nja), nja)
        remote(
            tn_in.at[slot3], tn_in.at[slot3], send_sem.at[15], recv_sem.at[15], dia, dja, ka
        ).start()

    @pl.loop(0, nia)
    def _(s):
        pair_copy(s).wait_send()

    slab_copy.wait_send()
    for place_, ref in (
        (0, ring_in),
        (1, gc_in.at[pl.ds(0, slots - 1)]),
        (2, gs_in.at[pl.ds(0, nja - 1)]),
        (3, gt_in.at[pl.ds(0, nka - 1)]),
        (5, ga_in.at[pl.ds(0, nia - 1)]),
        (6, sum_in.at[pl.ds(0, groups - 1)]),
        (7, fn_in.at[pl.ds(0, slots - 1)]),
        (8, gfa_in.at[pl.ds(0, nia - 1)]),
        (9, gfb_in.at[pl.ds(0, nia - 1)]),
        (10, ps_in.at[pl.ds(0, nka - 1)]),
        (11, pa_in.at[pl.ds(0, nia - 1)]),
        (12, sn_in.at[pl.ds(0, nka - 1)]),
        (13, gn_in.at[pl.ds(0, nja - 1)]),
        (14, ts_in.at[pl.ds(0, nia * nja - 1)]),
        (15, tn_in.at[pl.ds(0, nia * nja - 1)]),
    ):
        wait_bytes(ref, send_sem.at[place_])

    wait_bytes(tn_in.at[pl.ds(0, nia * nja - 1)], recv_sem.at[15])
    tn_t = tn_in[...].astype(F32).reshape(rank, tk).astype(BF16)
    time_out[...] = transposed(tn_t).astype(BF16)


def on_device(nia, nja, nka, tensor, matrix, first_factor, second_factor, time_factor, column_factor):
    ti, tj, tk = tensor.shape
    rank = first_factor.shape[1]
    depth = column_factor.shape[0]
    nyh = nja // 2
    slots = nja * nka
    q1, q2, q3 = rank // slots, rank // nka, rank // (nia * nja)
    groups = nka * nyh
    half = tj // 2
    V = pltpu.VMEM
    scratch = [
        V((ti, tj, tk), BF16),
        V((half, ti, 2 * tk), BF16),
        V((half, rank, 2 * tk), F32),
        V((nia, ti, depth), BF16),
        V((rank, depth), BF16),
        V((nia, 2, groups, q1, ti), F32),
        V((nia, groups, q1, ti), F32),
        V((nia - 1, groups, q1, ti), F32),
        V((ti, rank), F32),
        V((2, groups, q1, ti), F32),
        V((groups, q1, ti), F32),
        V((groups, q1, ti), F32),
        V((groups, q1, ti), F32),
        V((slots, q1, rank), F32),
        V((slots, q1, rank), F32),
        V((slots, q1, rank), F32),
        V((nja, q1, rank), F32),
        V((nka, q2, rank), F32),
        V((nka, q2, rank), F32),
        V((nja, q1, rank), F32),
        V((nia, q1, rank), F32),
        V((slots, q1, ti), F32),
        V((nka, q2, tj), F32),
        V((nia * nja, q3, tk), F32),
        V((tj, rank), F32),
        V((tk, rank), F32),
        V((slots, q1, ti), BF16),
        V((ti, rank), F32),
        V((nia * nja, q3, rank), F32),
        V((nia, q2 // q3, q3, rank), F32),
        V((nia, q3, rank), F32),
        V((tj, rank), F32),
        V((nka, q2, tj), F32),
        V((nka, q2, tj), F32),
        V((nia, q2, tj), F32),
        V((nka, q2, tj), BF16),
        V((nia, nja * q3, tj), BF16),
        V((nja, q3, rank), F32),
        V((nja, q3, rank), F32),
        V((rank, 2 * tk), F32),
        V((nia * nja, q3, tk), F32),
        V((nia * nja, q3, tk), F32),
        V((nia * nja, q3, tk), BF16),
        pltpu.SemaphoreType.DMA((nia,)),
        pltpu.SemaphoreType.DMA((ti // 16,)),
        pltpu.SemaphoreType.DMA((nia,)),
        pltpu.SemaphoreType.DMA((nia,)),
        pltpu.SemaphoreType.DMA((16,)),
        pltpu.SemaphoreType.DMA((16,)),
    ]
    in_vmem = pl.BlockSpec(memory_space=pltpu.VMEM)
    in_place = pl.BlockSpec(memory_space=pl.ANY)
    return pl.pallas_call(
        functools.partial(kernel, (nia, nja, nka, rank, ti, tj, tk)),
        out_shape=(
            jax.ShapeDtypeStruct((ti, rank), BF16),
            jax.ShapeDtypeStruct((tj, rank), BF16),
            jax.ShapeDtypeStruct((tk, rank), BF16),
        ),
        in_specs=[in_place, in_place, in_vmem, in_vmem, in_vmem, in_vmem],
        out_specs=(in_vmem, in_vmem, in_vmem),
        scratch_shapes=scratch,
        compiler_params=pltpu.CompilerParams(
            collective_id=0, has_side_effects=True, vmem_limit_bytes=60 * 1024 * 1024
        ),
        name="factor_round",
    )(tensor, matrix, first_factor, second_factor, time_factor, column_factor)


def solution(mesh):
    sizes = (mesh.shape["ia"], mesh.shape["ja"], mesh.shape["ka"])
    return jax.shard_map(
        functools.partial(on_device, *sizes),
        mesh=mesh,
        in_specs=(
            P("ia", "ja", "ka"),
            P(None, ("ia", "ja", "ka")),
            P("ia", None),
            P("ja", None),
            P("ka", None),
            P(("ia", "ja", "ka"), None),
        ),
        out_specs=(P("ia", None), P("ja", None), P("ka", None)),
        check_vma=False,
    )
```

time: 1290 us -> 98.2 us (0.08)
  waiting for transfers between devices: 1220 us -> 0 us
  Pallas kernels: 0 us -> 92.8 us
  matrix products: 31.9 us -> 0 us
  local copies, waits for them, and re-layouts: 18.4 us -> 4.51 us
  between operations: 13.9 us -> 0.64 us
    psum x4 -> x0, waiting for transfers between devices: 1220 us -> none  [the longest x1 540 us: on_device(): plane_sum, gram_first = lax.psum((plane_sum, gram_first), ('ia', 'ka'))]
    pallas_call x0 -> x1, Pallas kernels: none -> 92.8 us  [on_device(): pl.pallas_call(functools.partial(kernel, (nia, nja, nka, rank, ti, tj, tk...]
    dot_general x10 -> x0, matrix products: 20.4 us -> none  [the longest x1 6.45 us: on_device(): jnp.dot(tensor.reshape(tile_i, tile_j * tile_k), khatri, preferred_elemen...]
  transfers between devices with their start and end apart: 4 -> 0, of which waited for: 4 -> 0; matrix products, arithmetic and copies ran while one was open for 1% -> 0% of each run, Pallas kernels for 0% -> 0%
where the time goes in v1:
time: 98.2 us; the launch traced here: 98 us
  Pallas kernels  92.8 us (95%)
  local copies, waits for them, and re-layouts  4.51 us (5%)
    pallas_call x1, Pallas kernels, on_device(): pl.pallas_call(functools.partial(kernel, (nia, nja, nka, rank, ti, tj, tk...  92.8 us
    unnamed x3, local copies, waits for them, and re-layouts  4.51 us

profile of v1, /device:TPU:1, one launch (start us, length us, event | category | flops | bytes accessed | tf_op | source)
XLA Modules:
  0.0 98.0 jit_solution(1928565511691559842)
XLA Ops:
  0.6 92.8 %factor_round.1 = (bf16[256,256]{1,0:T(8,128)(2,1)}, bf16[128,256]{1,0:T(8,128)(2,1)}, bf16[128,256]{1,0:T(8,128)(2,1)}) custom-call(bf16[256,128,128]{2,1,0:T(8,128)(2,1)} %tensor_ref.1, bf16[2048,1024]{1,0:T(8,128)(2,1)} %matrix_ref.1, bf16[256,256]{1,0:T(8,128)(2,1)} %first_ref.1, bf16[128,256]{1,0:T(8,128)(2,1)} %second_ref.1, ...), custom_call_target="tpu_custom_call" | custom-call | tf_op jit(solution)/shard_map/factor_round/pallas_call | solution.py:538
  93.5 1.6 %copy.12 = bf16[256,256]{1,0:T(8,128)(2,1)} copy(bf16[256,256]{1,0:T(8,128)(2,1)} %get-tuple-element.6) | data formatting | bytes 262144
  95.1 1.5 %copy.13 = bf16[128,256]{1,0:T(8,128)(2,1)} copy(bf16[128,256]{1,0:T(8,128)(2,1)} %get-tuple-element.7) | data formatting | bytes 131072
  96.5 1.5 %copy.14 = bf16[128,256]{1,0:T(8,128)(2,1)} copy(bf16[128,256]{1,0:T(8,128)(2,1)} %get-tuple-element.8) | data formatting | bytes 131072

commit v2 on v1

--- a/solution.py
+++ b/solution.py
@@ -55,6 +55,7 @@
     time_out,
     tens,
     perm,
+    turn,
     wide,
     mats,
     col_t,
@@ -80,7 +81,6 @@
     second_f,
     time_f,
     fn_in,
-    fn_rows,
     gf_loc,
     gfa_in,
     gfb_in,
@@ -92,7 +92,7 @@
     sn_groups,
     gn_loc,
     gn_in,
-    tsum,
+    sn_f,
     ts_loc,
     ts_in,
     tn_in,
@@ -173,7 +173,6 @@
         )
 
     col_t[...] = transposed(column_ref[...]).astype(BF16)
-    pl.semaphore_wait(barrier, slots - 1 + (nia - 1) * nja)
 
     def pair_copy(s):
         return remote(
@@ -185,7 +184,6 @@
         block = dot_nt(col_t[...], mats[s]).reshape(groups, 2, q1, ti)
         coup[s, 0] = block[:, 0]
         coup[s, 1] = block[:, 1]
-        pair_copy(s).start()
 
     def paired_sum(s):
         pair_copy(s).wait_recv()
@@ -196,13 +194,9 @@
             coup.at[s, core], ring_in.at[s], send_sem.at[0], recv_sem.at[0], block_of(s), ja, ka
         )
 
-    coupled_block(0)
-
-    @pl.loop(1, nia)
+    @pl.loop(0, nia)
     def _(s):
         coupled_block(s)
-        paired_sum(s - 1)
-        ring_copy(s - 1).start()
 
     gc_loc[...] = dot(col_t[...], column_ref[...]).reshape(slots, q1, rank)
     time_tr = transposed(time_ref[...])
@@ -217,6 +211,16 @@
     gc_in[slot1] = gc_loc[slot1]
     gs_in[ja] = gs_loc[slot1]
     gt_in[ka] = gt_loc[ka]
+    pl.semaphore_wait(barrier, slots - 1 + (nia - 1) * nja)
+
+    @pl.loop(0, nia)
+    def _(s):
+        pair_copy(s).start()
+
+    @pl.loop(0, nia - 1)
+    def _(s):
+        paired_sum(s)
+        ring_copy(s).start()
 
     @pl.loop(1, slots)
     def _(t):
@@ -276,6 +280,14 @@
     )
     slab_copy.start()
 
+    unit = identity(2 * tk)
+
+    def turn_blocks(start, stop):
+        @pl.loop(start, stop)
+        def _(b):
+            for u in range(4):
+                turn[4 * b + u] = dot_nt(unit, perm[4 * b + u]).astype(BF16)
+
     wait_bytes(gc_in.at[pl.ds(0, slots - 1)], recv_sem.at[1])
     ga_in[ia] = jnp.sum(gc_in[...], axis=0)
 
@@ -310,6 +322,7 @@
             dka,
         ).start()
 
+    turn_blocks(0, half // 8)
     wait_bytes(ga_in.at[pl.ds(0, nia - 1)], recv_sem.at[5])
     gram_total = gram_part + jnp.sum(ga_in[...], axis=0)
     denominator = exact_product(gram_total, first_ref[...])
@@ -324,10 +337,10 @@
             fn_in.at[slot1], fn_in.at[slot1], send_sem.at[7], recv_sem.at[7], ia, dja, dka
         ).start()
 
+    turn_blocks(half // 8, half // 4)
     wait_bytes(fn_in.at[pl.ds(0, slots - 1)], recv_sem.at[7])
     fn_t = fn_in[...].astype(F32).reshape(rank, ti).astype(BF16)
-    fn_rows[...] = transposed(fn_t)
-    fn = fn_rows[...].astype(BF16)
+    fn = transposed(fn_t).astype(BF16)
     first_out[...] = fn
     gf_loc[...] = dot(fn_t, fn).reshape(nia * nja, q3, rank)
     ratio = q2 // q3
@@ -343,17 +356,15 @@
             gf_loc.at[dia * nja + ja], gfb_in.at[ia], send_sem.at[9], recv_sem.at[9], dia, ja, ka
         ).start()
 
-    plane[...] = jnp.zeros_like(plane)
-
-    @pl.loop(0, ti // 8)
+    @pl.loop(0, half // 4)
     def _(b):
-        i0 = pl.multiple_of(b * 8, 8)
-        block = dot(tens[pl.ds(i0, 8)].reshape(8 * tj, tk), time_ref[...]).reshape(8, tj, rank)
-        scaled = fn_rows[pl.ds(i0, 8), :]
-        total = plane[...]
-        for u in range(8):
-            total = total + block[u] * scaled[u : u + 1, :]
-        plane[...] = total
+        for u in range(4):
+            j = b * 4 + u
+            block = dot(turn[j], first_out[...])
+            wide[j] = block
+            sums = jnp.sum(block.reshape(2, tk, rank) * time_f[...][None], axis=1)
+            plane[pl.ds(j, 1), :] = sums[0:1]
+            plane[pl.ds(j + half, 1), :] = sums[1:2]
 
     ps_loc[...] = plane[...].T.reshape(nka, q2, tj)
     ps_in[ka] = ps_loc[ka]
@@ -363,12 +374,6 @@
         dka = wrap(ka + t, nka)
         remote(ps_loc.at[dka], ps_in.at[ka], send_sem.at[10], recv_sem.at[10], ia, ja, dka).start()
 
-    def weigh(start, stop):
-        @pl.loop(start, stop)
-        def _(j):
-            wide[j] = dot(fn_in[...].astype(F32).reshape(rank, ti).astype(BF16), perm[j])
-
-    weigh(0, half // 2)
     wait_bytes(ps_in.at[pl.ds(0, nka - 1)], recv_sem.at[10])
     pa_in[ia] = jnp.sum(ps_in[...], axis=0)
 
@@ -381,7 +386,6 @@
     wait_bytes(gfa_in.at[pl.ds(0, nia - 1)], recv_sem.at[8])
     gram_rows = jnp.sum(gfa_in[...], axis=0).reshape(q2, rank) * gt_sum[...].reshape(q2, rank)
     second_den = exact_product(gram_rows, second_ref[...])
-    weigh(half // 2, half)
     wait_bytes(pa_in.at[pl.ds(0, nia - 1)], recv_sem.at[11])
     second_num = jnp.sum(pa_in[...], axis=0)
     sn_in[ka] = (second_t[ka] * second_num / second_den).astype(BF16)
@@ -403,21 +407,19 @@
         dja = wrap(ja + t, nja)
         remote(gn_loc.at[dja], gn_in.at[ja], send_sem.at[13], recv_sem.at[13], ia, dja, ka).start()
 
-    tsum[...] = jnp.zeros_like(tsum)
-    lane = lax.broadcasted_iota(jnp.int32, (tj, 2 * tk), 1) // tk
-    row = lax.broadcasted_iota(jnp.int32, (tj, 2 * tk), 0)
-    place = row - lane * half
-
-    @pl.loop(0, half // 4)
-    def _(b):
-        total = tsum[...]
+    sn_rows = transposed(sn_t)
+    second_out[...] = sn_rows.astype(BF16)
+    sn_f[...] = sn_rows
+
+    def add_planes(b, total):
         for u in range(4):
             j = b * 4 + u
-            pick = (place == j).astype(F32).astype(BF16)
-            total = total + dot(sn_t, pick) * wide[j]
-        tsum[...] = total
-
-    ts_loc[...] = (tsum[:, :tk] + tsum[:, tk:]).reshape(nia * nja, q3, tk)
+            total = total + wide[j, :tk] * sn_f[pl.ds(j, 1), :]
+            total = total + wide[j, tk:] * sn_f[pl.ds(j + half, 1), :]
+        return total
+
+    tsum = lax.fori_loop(0, half // 4, add_planes, jnp.zeros((tk, rank), F32))
+    ts_loc[...] = tsum.T.reshape(nia * nja, q3, tk)
     ts_in[slot3] = ts_loc[slot3]
 
     @pl.loop(1, nia * nja)
@@ -427,7 +429,6 @@
             ts_loc.at[dia * nja + dja], ts_in.at[slot3], send_sem.at[14], recv_sem.at[14], dia, dja, ka
         ).start()
 
-    second_out[...] = transposed(sn_t).astype(BF16)
     wait_bytes(gfb_in.at[pl.ds(0, nia - 1)], recv_sem.at[9])
     wait_bytes(gn_in.at[pl.ds(0, nja - 1)], recv_sem.at[13])
     gram_rows = jnp.sum(gfb_in[...], axis=0) * jnp.sum(gn_in[...], axis=0)
@@ -472,6 +473,15 @@
     time_out[...] = transposed(tn_t).astype(BF16)
 
 
+def hand_out(first, second, time, first_out, second_out, time_out, sem):
+    pairs = ((first, first_out), (second, second_out), (time, time_out))
+    copies = [pltpu.make_async_copy(a, b, sem.at[n]) for n, (a, b) in enumerate(pairs)]
+    for copy in copies:
+        copy.start()
+    for copy in copies:
+        copy.wait()
+
+
 def on_device(nia, nja, nka, tensor, matrix, first_factor, second_factor, time_factor, column_factor):
     ti, tj, tk = tensor.shape
     rank = first_factor.shape[1]
@@ -485,7 +495,8 @@
     scratch = [
         V((ti, tj, tk), BF16),
         V((half, ti, 2 * tk), BF16),
-        V((half, rank, 2 * tk), F32),
+        V((half, 2 * tk, ti), BF16),
+        V((half, 2 * tk, rank), F32),
         V((nia, ti, depth), BF16),
         V((rank, depth), BF16),
         V((nia, 2, groups, q1, ti), F32),
@@ -510,7 +521,6 @@
         V((tj, rank), F32),
         V((tk, rank), F32),
         V((slots, q1, ti), BF16),
-        V((ti, rank), F32),
         V((nia * nja, q3, rank), F32),
         V((nia, q2 // q3, q3, rank), F32),
         V((nia, q3, rank), F32),
@@ -522,7 +532,7 @@
         V((nia, nja * q3, tj), BF16),
         V((nja, q3, rank), F32),
         V((nja, q3, rank), F32),
-        V((rank, 2 * tk), F32),
+        V((tj, rank), F32),
         V((nia * nja, q3, tk), F32),
         V((nia * nja, q3, tk), F32),
         V((nia * nja, q3, tk), BF16),
@@ -535,13 +545,14 @@
     ]
     in_vmem = pl.BlockSpec(memory_space=pltpu.VMEM)
     in_place = pl.BlockSpec(memory_space=pl.ANY)
-    return pl.pallas_call(
+    shapes = (
+        jax.ShapeDtypeStruct((ti, rank), BF16),
+        jax.ShapeDtypeStruct((tj, rank), BF16),
+        jax.ShapeDtypeStruct((tk, rank), BF16),
+    )
+    results = pl.pallas_call(
         functools.partial(kernel, (nia, nja, nka, rank, ti, tj, tk)),
-        out_shape=(
-            jax.ShapeDtypeStruct((ti, rank), BF16),
-            jax.ShapeDtypeStruct((tj, rank), BF16),
-            jax.ShapeDtypeStruct((tk, rank), BF16),
-        ),
+        out_shape=shapes,
         in_specs=[in_place, in_place, in_vmem, in_vmem, in_vmem, in_vmem],
         out_specs=(in_vmem, in_vmem, in_vmem),
         scratch_shapes=scratch,
@@ -550,6 +561,14 @@
         ),
         name="factor_round",
     )(tensor, matrix, first_factor, second_factor, time_factor, column_factor)
+    return pl.pallas_call(
+        hand_out,
+        out_shape=shapes,
+        in_specs=[in_place] * 3,
+        out_specs=(in_place,) * 3,
+        scratch_shapes=[pltpu.SemaphoreType.DMA((3,))],
+        name="hand_out",
+    )(*results)
 
 
 def solution(mesh):

time: 98.2 us -> 91.4 us (0.931)
  local copies, waits for them, and re-layouts: 4.51 us -> 0 us
  Pallas kernels: 92.8 us -> 90.7 us
    pallas_call x1, Pallas kernels: 92.8 us -> 81.6 us  [on_device(): pl.pallas_call(functools.partial(kernel, (nia, nja, nka, rank, ti, tj, tk...]
    pallas_call x0 -> x1, Pallas kernels: none -> 9.07 us  [on_device(): pl.pallas_call(hand_out, out_shape=shapes, in_specs=[in_place] * 3, out_s...]
    unnamed x3 -> x0, local copies, waits for them, and re-layouts: 4.51 us -> none
where the time goes in v2:
time: 91.4 us; the launch traced here: 91.3 us
  Pallas kernels  90.7 us (99%)
    pallas_call x1, Pallas kernels, on_device(): pl.pallas_call(functools.partial(kernel, (nia, nja, nka, rank, ti, tj, tk...  81.6 us
    pallas_call x1, Pallas kernels, on_device(): pl.pallas_call(hand_out, out_shape=shapes, in_specs=[in_place] * 3, out_s...  9.07 us

profile of v2, /device:TPU:1, one launch (start us, length us, event | category | flops | bytes accessed | tf_op | source)
XLA Modules:
  0.0 91.3 jit_solution(6205707508588004401)
XLA Ops:
  0.6 81.6 %factor_round.1 = (bf16[256,256]{1,0:T(8,128)(2,1)}, bf16[128,256]{1,0:T(8,128)(2,1)}, bf16[128,256]{1,0:T(8,128)(2,1)}) custom-call(bf16[256,128,128]{2,1,0:T(8,128)(2,1)} %tensor_ref.1, bf16[2048,1024]{1,0:T(8,128)(2,1)} %matrix_ref.1, bf16[256,256]{1,0:T(8,128)(2,1)} %first_ref.1, bf16[128,256]{1,0:T(8,128)(2,1)} %second_ref.1, ...), custom_call_target="tpu_custom_call" | custom-call | tf_op jit(solution)/shard_map/factor_round/pallas_call | solution.py:553
  82.2 9.1 %hand_out.1 = (bf16[256,256]{1,0:T(8,128)(2,1)}, bf16[128,256]{1,0:T(8,128)(2,1)}, bf16[128,256]{1,0:T(8,128)(2,1)}) custom-call(bf16[256,256]{1,0:T(8,128)(2,1)} %get-tuple-element.6.first, bf16[128,256]{1,0:T(8,128)(2,1)} %get-tuple-element.7.second, bf16[128,256]{1,0:T(8,128)(2,1)} %get-tuple-element.8.time), custom_call_target="tpu_custom_call" | custom-call | tf_op jit(solution)/shard_map/hand_out/pallas_call | solution.py:564

commit v3 on v2

v3 whole, which is shorter than its diff:
```python
import functools

import jax
import jax.numpy as jnp
from jax import lax
from jax.experimental import pallas as pl
from jax.experimental.pallas import tpu as pltpu
from jax.sharding import PartitionSpec as P

F32 = jnp.float32
BF16 = jnp.bfloat16


def dot(a, b):
    return jnp.dot(a, b, preferred_element_type=F32)


def dot_nt(a, b):
    return lax.dot_general(a, b, (((1,), (1,)), ((), ())), preferred_element_type=F32)


def identity(n):
    rows = lax.broadcasted_iota(jnp.int32, (n, n), 0)
    columns = lax.broadcasted_iota(jnp.int32, (n, n), 1)
    return (rows == columns).astype(F32).astype(BF16)


def transposed(values):
    return dot_nt(identity(values.shape[1]), values)


def exact_product(gram, factor):
    rows = gram.shape[0]
    high = gram.astype(BF16).astype(F32)
    rest = gram - high
    middle = rest.astype(BF16).astype(F32)
    low = (rest - middle).astype(BF16).astype(F32)
    parts = [high, middle, low]
    while (rows * len(parts)) % 16:
        parts.append(jnp.zeros_like(high))
    stacked = dot_nt(jnp.concatenate(parts, axis=0).astype(BF16), factor)
    return stacked[:rows] + (stacked[rows : 2 * rows] + stacked[2 * rows : 3 * rows])


def kernel(
    sizes,
    tensor_ref,
    matrix_ref,
    first_ref,
    second_ref,
    time_ref,
    column_ref,
    first_out,
    second_out,
    time_out,
    tens,
    perm,
    turn,
    wide,
    mats,
    col_t,
    coup,
    pair_in,
    ring_in,
    slab_acc,
    slab_half,
    slab_in,
    sum_half,
    sum_in,
    gc_loc,
    gc_pair,
    gc_half,
    gc_in,
    gs_loc,
    gs_in,
    gt_loc,
    gt_in,
    gt_wide,
    ga_in,
    first_t,
    second_t,
    time_t,
    second_f,
    time_f,
    fn_in,
    gf_loc,
    gf_in,
    gf_sum,
    plane,
    ps_loc,
    ps_in,
    pa_in,
    sn_in,
    gn_loc,
    gn_in,
    sn_f,
    ts_loc,
    ts_in,
    tn_in,
    mat_sem,
    tens_sem,
    pair_send,
    pair_recv,
    send_sem,
    recv_sem,
):
    nia, nja, nka, rank, ti, tj, tk = sizes
    nyh = nja // 2
    nx = nia // 2
    slots = nja * nka
    q1, q3 = rank // slots, rank // (nia * nja)
    q4 = nja * q3
    groups = nka * nyh
    half = tj // 2
    ia, ja, ka = lax.axis_index("ia"), lax.axis_index("ja"), lax.axis_index("ka")
    core = lax.rem(ja, 2)
    other = 1 - core
    yh = ja // 2
    slot1 = ka * nja + ja
    group = ka * nyh + yh
    slot3 = ia * nja + ja

    def wrap(value, n):
        return lax.rem(value + n, n)

    def far(u, n):
        return n // 2 + (1 - 2 * lax.rem(u, 2)) * ((u + 1) // 2)

    def ia_of(u):
        row = wrap(ia // nx + 1 - u // nx, 2)
        return row * nx + wrap(lax.rem(ia, nx) + far(lax.rem(u, nx), nx), nx)

    def ka_of(u):
        return wrap(ka + far(u, nka), nka)

    def group_of(t):
        return wrap(yh + nyh - 1 - lax.rem(t, nyh), nyh), ka_of(t // nyh)

    def plane_of(t):
        return ia_of(t // nja), wrap(ja + far(lax.rem(t, nja), nja), nja)

    def remote(src, dst, s_sem, r_sem, dia, dja, dka):
        return pltpu.make_async_remote_copy(
            src_ref=src,
            dst_ref=dst,
            send_sem=s_sem,
            recv_sem=r_sem,
            device_id=(dia, dja, dka),
            device_id_type=pl.DeviceIdType.MESH,
        )

    def wait_bytes(ref, sem):
        pltpu.make_async_copy(ref, ref, sem).wait()

    sibling = ja + 1 - 2 * core
    block_of = ia_of

    def mat_copy(s):
        rows = pl.ds(pl.multiple_of(block_of(s) * ti, ti), ti)
        return pltpu.make_async_copy(matrix_ref.at[rows, :], mats.at[s], mat_sem.at[s])

    def tens_copy(b):
        rows = pl.ds(b * 16, 16)
        return pltpu.make_async_copy(tensor_ref.at[rows], tens.at[rows], tens_sem.at[b])

    @pl.loop(0, nia)
    def _(s):
        mat_copy(s).start()

    @pl.loop(0, ti // 16)
    def _(b):
        tens_copy(b).start()

    barrier = pltpu.get_barrier_semaphore()

    def greet(dia, dja, dka):
        pl.semaphore_signal(
            barrier, inc=1, device_id=(dia, dja, dka), device_id_type=pl.DeviceIdType.MESH
        )

    @pl.loop(0, groups - 1)
    def _(t):
        dyh, dka = group_of(t)
        greet(ia, 2 * dyh + core, dka)

    @pl.loop(0, (nia - 1) * nja)
    def _(t):
        dia, dja = plane_of(t)
        greet(dia, dja, ka)

    greet(ia, 2 * (1 - yh) + other, ka)
    greet(ia, sibling, ka)
    col_t[...] = transposed(column_ref[...]).astype(BF16)

    def pair_copy(s):
        return remote(
            coup.at[s, other], pair_in.at[s], pair_send.at[s], pair_recv.at[s], ia, sibling, ka
        )

    def coupled_block(s):
        mat_copy(s).wait()
        block = dot_nt(col_t[...], mats[s]).reshape(groups, 2, q1, ti)
        coup[s, 0] = block[:, 0]
        coup[s, 1] = block[:, 1]

    def paired_sum(s):
        pair_copy(s).wait_recv()
        coup[s, core] = coup[s, core] + pair_in[s]

    def ring_copy(s):
        return remote(
            coup.at[s, core], ring_in.at[s], send_sem.at[0], recv_sem.at[0], block_of(s), ja, ka
        )

    @pl.loop(0, nia)
    def _(s):
        coupled_block(s)

    pl.semaphore_wait(barrier, groups - 1 + (nia - 1) * nja + 2)

    @pl.loop(0, nia)
    def _(s):
        pair_copy(s).start()

    gram = dot(col_t[...], column_ref[...]).reshape(groups, 2, q1, rank)
    gc_loc[0] = gram[:, 0]
    gc_loc[1] = gram[:, 1]
    gc_copy = remote(gc_loc.at[other], gc_pair, send_sem.at[9], recv_sem.at[9], ia, sibling, ka)
    gc_copy.start()

    @pl.loop(0, nia - 1)
    def _(s):
        paired_sum(s)
        ring_copy(s).start()

    time_tr = transposed(time_ref[...])
    time_t[...] = time_tr.reshape(nia * nja, q3, tk)
    gt_loc[...] = dot(time_tr.astype(BF16), time_ref[...]).reshape(slots, q1, rank)
    mine = pl.ds(ia * (q4 // q1), q4 // q1)
    gt_in[ka] = gt_loc[slot1]
    gt_wide[ka] = gt_loc[mine]

    @pl.loop(0, nka - 1)
    def _(t):
        dka = ka_of(t)
        remote(
            gt_loc.at[dka * nja + ja], gt_in.at[ka], send_sem.at[3], recv_sem.at[3], ia, ja, dka
        ).start()
        remote(gt_loc.at[mine], gt_wide.at[ka], send_sem.at[8], recv_sem.at[8], ia, ja, dka).start()

    gc_copy.wait_recv()
    gc_half[...] = gc_loc[core] + gc_pair[...]
    gc_in[group] = gc_half[group]

    @pl.loop(0, groups - 1)
    def _(t):
        dyh, dka = group_of(t)
        remote(
            gc_half.at[dka * nyh + dyh],
            gc_in.at[group],
            send_sem.at[1],
            recv_sem.at[1],
            ia,
            2 * dyh + core,
            dka,
        ).start()

    second_tr = transposed(second_ref[...])
    second_t[...] = second_tr.reshape(nia, q4, tj)
    gs_loc[...] = dot(second_tr.astype(BF16), second_ref[...]).reshape(slots, q1, rank)
    gs_in[ja] = gs_loc[slot1]

    @pl.loop(1, nja)
    def _(t):
        dja = wrap(ja + t, nja)
        remote(
            gs_loc.at[ka * nja + dja], gs_in.at[ja], send_sem.at[2], recv_sem.at[2], ia, dja, ka
        ).start()

    first_t[...] = transposed(first_ref[...]).reshape(slots, q1, ti)
    second_f[...] = second_ref[...].astype(F32)
    time_f[...] = time_ref[...].astype(F32)
    paired_sum(nia - 1)

    rows = lax.broadcasted_iota(jnp.int32, (256, 256), 0)
    columns = lax.broadcasted_iota(jnp.int32, (256, 256), 1)
    order = (lax.rem(rows, 16) == columns // 16) & (rows // 16 == lax.rem(columns, 16))
    order = order.astype(F32).astype(BF16)

    @pl.loop(0, ti // 16)
    def _(b):
        tens_copy(b).wait()
        i0 = pl.multiple_of(b * 16, 16)
        for c in range(half // 16):
            low = tens[pl.ds(i0, 16), 16 * c : 16 * c + 16, :].reshape(256, tk)
            high = tens[pl.ds(i0, 16), half + 16 * c : half + 16 * c + 16, :].reshape(256, tk)
            block = dot(order, jnp.concatenate([low, high], axis=1))
            perm[16 * c : 16 * c + 16, pl.ds(i0, 16), :] = block.astype(BF16).reshape(16, 16, 2 * tk)

    slab_acc[...] = jnp.zeros_like(slab_acc)

    @pl.loop(0, half // 4)
    def _(b):
        total = slab_acc[...]
        for u in range(4):
            j = b * 4 + u
            khatri = jnp.concatenate(
                [time_f[...] * second_f[pl.ds(j, 1), :], time_f[...] * second_f[pl.ds(j + half, 1), :]],
                axis=0,
            ).astype(BF16)
            total = total + dot(perm[j], khatri)
        slab_acc[...] = total

    slab_tr = slab_acc[...].T.reshape(groups, 2, q1, ti)
    slab_half[0] = slab_tr[:, 0]
    slab_half[1] = slab_tr[:, 1]
    slab_copy = remote(
        slab_half.at[other], slab_in, send_sem.at[4], recv_sem.at[4], ia, sibling, ka
    )
    slab_copy.start()

    unit = identity(2 * tk)

    def turn_blocks(start, stop):
        @pl.loop(start, stop)
        def _(b):
            for u in range(4):
                turn[4 * b + u] = dot_nt(unit, perm[4 * b + u]).astype(BF16)

    wait_bytes(gc_in.at[pl.ds(0, groups - 1)], recv_sem.at[1])
    ga_in[ia] = jnp.sum(gc_in[...], axis=0)

    @pl.loop(0, nia - 1)
    def _(t):
        remote(ga_in.at[ia], ga_in.at[ia], send_sem.at[5], recv_sem.at[5], ia_of(t), ja, ka).start()

    wait_bytes(gs_in.at[pl.ds(0, nja - 1)], recv_sem.at[2])
    wait_bytes(gt_in.at[pl.ds(0, nka - 1)], recv_sem.at[3])
    gram_part = jnp.sum(gs_in[...], axis=0) * jnp.sum(gt_in[...], axis=0)

    wait_bytes(ring_in, recv_sem.at[0])
    slab_copy.wait_recv()
    sum_half[...] = (
        coup[nia - 1, core] + jnp.sum(ring_in[...], axis=0) + (slab_half[core] + slab_in[...])
    )
    sum_in[group] = sum_half[group]

    @pl.loop(0, groups - 1)
    def _(t):
        dyh, dka = group_of(t)
        remote(
            sum_half.at[dka * nyh + dyh],
            sum_in.at[group],
            send_sem.at[6],
            recv_sem.at[6],
            ia,
            2 * dyh + core,
            dka,
        ).start()

    turn_blocks(0, half // 8)
    wait_bytes(ga_in.at[pl.ds(0, nia - 1)], recv_sem.at[5])
    gram_total = gram_part + jnp.sum(ga_in[...], axis=0)
    denominator = exact_product(gram_total, first_ref[...])
    wait_bytes(sum_in.at[pl.ds(0, groups - 1)], recv_sem.at[6])
    numerator = jnp.sum(sum_in[...], axis=0)
    fn_in[core, group] = (first_t[slot1] * numerator / denominator).astype(BF16)

    @pl.loop(0, groups - 1)
    def _(t):
        dyh, dka = group_of(t)
        remote(
            fn_in.at[core, group],
            fn_in.at[core, group],
            send_sem.at[7],
            recv_sem.at[7],
            ia,
            2 * dyh + core,
            dka,
        ).start()

    turn_blocks(half // 8, half // 4)
    wait_bytes(fn_in.at[0, pl.ds(0, groups - 1)], recv_sem.at[7])
    fn_copy = remote(fn_in.at[core], fn_in.at[core], send_sem.at[12], recv_sem.at[12], ia, sibling, ka)
    fn_copy.start()
    wait_bytes(gt_wide.at[pl.ds(0, nka - 1)], recv_sem.at[8])
    gt_rows = jnp.sum(gt_wide[...], axis=0).reshape(q4, rank)
    fn_copy.wait_recv()
    fn_t = jnp.stack([fn_in[0].astype(F32), fn_in[1].astype(F32)], axis=1)
    fn_t = fn_t.reshape(rank, ti).astype(BF16)
    fn = transposed(fn_t).astype(BF16)
    first_out[...] = fn
    gf_loc[...] = dot(fn_t, fn).reshape(nia, q4, rank)
    gf_in[ia] = gf_loc[ia]

    @pl.loop(0, nia - 1)
    def _(t):
        dia = ia_of(t)
        remote(gf_loc.at[dia], gf_in.at[ia], send_sem.at[16], recv_sem.at[16], dia, ja, ka).start()

    @pl.loop(0, half // 4)
    def _(b):
        for u in range(4):
            j = b * 4 + u
            block = dot(turn[j], first_out[...])
            wide[j] = block
            sums = jnp.sum(block.reshape(2, tk, rank) * time_f[...][None], axis=1)
            plane[pl.ds(j, 1), :] = sums[0:1]
            plane[pl.ds(j + half, 1), :] = sums[1:2]

    ps_loc[...] = plane[...].T.reshape(nia, q4, tj)
    ps_in[ia] = ps_loc[ia]

    @pl.loop(0, nia - 1)
    def _(t):
        dia = ia_of(t)
        remote(ps_loc.at[dia], ps_in.at[ia], send_sem.at[10], recv_sem.at[10], dia, ja, ka).start()

    wait_bytes(ps_in.at[pl.ds(0, nia - 1)], recv_sem.at[10])
    pa_in[ka] = jnp.sum(ps_in[...], axis=0)

    @pl.loop(0, nka - 1)
    def _(t):
        remote(pa_in.at[ka], pa_in.at[ka], send_sem.at[11], recv_sem.at[11], ia, ja, ka_of(t)).start()

    wait_bytes(gf_in.at[pl.ds(0, nia - 1)], recv_sem.at[16])
    gf_rows = jnp.sum(gf_in[...], axis=0)
    gf_sum[...] = gf_rows.reshape(nja, q3, rank)
    second_den = exact_product(gf_rows * gt_rows, second_ref[...])
    second_mine = second_t[ia]
    wait_bytes(pa_in.at[pl.ds(0, nka - 1)], recv_sem.at[11])
    second_num = jnp.sum(pa_in[...], axis=0)
    sn_in[ia] = (second_mine * second_num / second_den).astype(BF16)

    @pl.loop(0, nia - 1)
    def _(t):
        remote(sn_in.at[ia], sn_in.at[ia], send_sem.at[17], recv_sem.at[17], ia_of(t), ja, ka).start()

    wait_bytes(sn_in.at[pl.ds(0, nia - 1)], recv_sem.at[17])
    sn_t = sn_in[...].reshape(rank, tj)
    gn_loc[...] = dot_nt(sn_in[ia], sn_t).reshape(nja, q3, rank)
    gn_in[ja] = gn_loc[ja]

    @pl.loop(1, nja)
    def _(t):
        dja = wrap(ja + t, nja)
        remote(gn_loc.at[dja], gn_in.at[ja], send_sem.at[13], recv_sem.at[13], ia, dja, ka).start()

    sn_rows = transposed(sn_t)
    second_out[...] = sn_rows.astype(BF16)
    sn_f[...] = sn_rows

    def add_planes(b, total):
        for u in range(4):
            j = b * 4 + u
            total = total + wide[j, :tk] * sn_f[pl.ds(j, 1), :]
            total = total + wide[j, tk:] * sn_f[pl.ds(j + half, 1), :]
        return total

    tsum = lax.fori_loop(0, half // 4, add_planes, jnp.zeros((tk, rank), F32))
    ts_loc[...] = tsum.T.reshape(nia * nja, q3, tk)
    ts_in[slot3] = ts_loc[slot3]

    @pl.loop(0, nia * nja - 1)
    def _(t):
        dia, dja = plane_of(t)
        remote(
            ts_loc.at[dia * nja + dja], ts_in.at[slot3], send_sem.at[14], recv_sem.at[14], dia, dja, ka
        ).start()

    wait_bytes(gn_in.at[pl.ds(0, nja - 1)], recv_sem.at[13])
    gram_rows = gf_sum[ja] * jnp.sum(gn_in[...], axis=0)
    time_den = exact_product(gram_rows, time_ref[...])
    wait_bytes(ts_in.at[pl.ds(0, nia * nja - 1)], recv_sem.at[14])
    time_num = jnp.sum(ts_in[...], axis=0)
    tn_in[slot3] = (time_t[slot3] * time_num / time_den).astype(BF16)

    @pl.loop(0, nia * nja - 1)
    def _(t):
        dia, dja = plane_of(t)
        remote(
            tn_in.at[slot3], tn_in.at[slot3], send_sem.at[15], recv_sem.at[15], dia, dja, ka
        ).start()

    @pl.loop(0, nia)
    def _(s):
        pair_copy(s).wait_send()

    slab_copy.wait_send()
    gc_copy.wait_send()
    fn_copy.wait_send()
    for place_, ref in (
        (0, ring_in),
        (1, gc_in.at[pl.ds(0, groups - 1)]),
        (2, gs_in.at[pl.ds(0, nja - 1)]),
        (3, gt_in.at[pl.ds(0, nka - 1)]),
        (5, ga_in.at[pl.ds(0, nia - 1)]),
        (6, sum_in.at[pl.ds(0, groups - 1)]),
        (7, fn_in.at[0, pl.ds(0, groups - 1)]),
        (8, gt_wide.at[pl.ds(0, nka - 1)]),
        (10, ps_in.at[pl.ds(0, nia - 1)]),
        (11, pa_in.at[pl.ds(0, nka - 1)]),
        (13, gn_in.at[pl.ds(0, nja - 1)]),
        (14, ts_in.at[pl.ds(0, nia * nja - 1)]),
        (15, tn_in.at[pl.ds(0, nia * nja - 1)]),
        (16, gf_in.at[pl.ds(0, nia - 1)]),
        (17, sn_in.at[pl.ds(0, nia - 1)]),
    ):
        wait_bytes(ref, send_sem.at[place_])

    wait_bytes(tn_in.at[pl.ds(0, nia * nja - 1)], recv_sem.at[15])
    tn_t = tn_in[...].astype(F32).reshape(rank, tk).astype(BF16)
    time_out[...] = transposed(tn_t).astype(BF16)


def hand_out(first, second, time, first_out, second_out, time_out):
    first_out[...] = first[...]
    second_out[...] = second[...]
    time_out[...] = time[...]


def on_device(nia, nja, nka, tensor, matrix, first_factor, second_factor, time_factor, column_factor):
    ti, tj, tk = tensor.shape
    rank = first_factor.shape[1]
    depth = column_factor.shape[0]
    nyh = nja // 2
    slots = nja * nka
    q1, q3 = rank // slots, rank // (nia * nja)
    q4 = nja * q3
    groups = nka * nyh
    half = tj // 2
    V = pltpu.VMEM
    scratch = [
        V((ti, tj, tk), BF16),
        V((half, ti, 2 * tk), BF16),
        V((half, 2 * tk, ti), BF16),
        V((half, 2 * tk, rank), F32),
        V((nia, ti, depth), BF16),
        V((rank, depth), BF16),
        V((nia, 2, groups, q1, ti), F32),
        V((nia, groups, q1, ti), F32),
        V((nia - 1, groups, q1, ti), F32),
        V((ti, rank), F32),
        V((2, groups, q1, ti), F32),
        V((groups, q1, ti), F32),
        V((groups, q1, ti), F32),
        V((groups, q1, ti), F32),
        V((2, groups, q1, rank), F32),
        V((groups, q1, rank), F32),
        V((groups, q1, rank), F32),
        V((groups, q1, rank), F32),
        V((slots, q1, rank), F32),
        V((nja, q1, rank), F32),
        V((slots, q1, rank), F32),
        V((nka, q1, rank), F32),
        V((nka, q4 // q1, q1, rank), F32),
        V((nia, q1, rank), F32),
        V((slots, q1, ti), F32),
        V((nia, q4, tj), F32),
        V((nia * nja, q3, tk), F32),
        V((tj, rank), F32),
        V((tk, rank), F32),
        V((2, groups, q1, ti), BF16),
        V((nia, q4, rank), F32),
        V((nia, q4, rank), F32),
        V((nja, q3, rank), F32),
        V((tj, rank), F32),
        V((nia, q4, tj), F32),
        V((nia, q4, tj), F32),
        V((nka, q4, tj), F32),
        V((nia, q4, tj), BF16),
        V((nja, q3, rank), F32),
        V((nja, q3, rank), F32),
        V((tj, rank), F32),
        V((nia * nja, q3, tk), F32),
        V((nia * nja, q3, tk), F32),
        V((nia * nja, q3, tk), BF16),
        pltpu.SemaphoreType.DMA((nia,)),
        pltpu.SemaphoreType.DMA((ti // 16,)),
        pltpu.SemaphoreType.DMA((nia,)),
        pltpu.SemaphoreType.DMA((nia,)),
        pltpu.SemaphoreType.DMA((18,)),
        pltpu.SemaphoreType.DMA((18,)),
    ]
    in_vmem = pl.BlockSpec(memory_space=pltpu.VMEM)
    in_place = pl.BlockSpec(memory_space=pl.ANY)
    shapes = (
        jax.ShapeDtypeStruct((ti, rank), BF16),
        jax.ShapeDtypeStruct((tj, rank), BF16),
        jax.ShapeDtypeStruct((tk, rank), BF16),
    )
    results = pl.pallas_call(
        functools.partial(kernel, (nia, nja, nka, rank, ti, tj, tk)),
        out_shape=shapes,
        in_specs=[in_place, in_place, in_vmem, in_vmem, in_vmem, in_vmem],
        out_specs=(in_vmem, in_vmem, in_vmem),
        scratch_shapes=scratch,
        compiler_params=pltpu.CompilerParams(
            collective_id=0, has_side_effects=True, vmem_limit_bytes=60 * 1024 * 1024
        ),
        name="factor_round",
    )(tensor, matrix, first_factor, second_factor, time_factor, column_factor)
    return pl.pallas_call(
        hand_out,
        out_shape=shapes,
        in_specs=[in_vmem] * 3,
        out_specs=(in_vmem,) * 3,
        name="hand_out",
    )(*results)


def solution(mesh):
    sizes = (mesh.shape["ia"], mesh.shape["ja"], mesh.shape["ka"])
    return jax.shard_map(
        functools.partial(on_device, *sizes),
        mesh=mesh,
        in_specs=(
            P("ia", "ja", "ka"),
            P(None, ("ia", "ja", "ka")),
            P("ia", None),
            P("ja", None),
            P("ka", None),
            P(("ia", "ja", "ka"), None),
        ),
        out_specs=(P("ia", None), P("ja", None), P("ka", None)),
        check_vma=False,
    )
```

time: 91.4 us -> 79.9 us (0.87)
  Pallas kernels: 90.7 us -> 79.1 us
    pallas_call x1, Pallas kernels: 9.07 us -> 1.65 us  [on_device(): pl.pallas_call(hand_out, out_shape=shapes, in_specs=[in_vmem] * 3, out_sp...]
    pallas_call x1, Pallas kernels: 81.6 us -> 77.5 us  [on_device(): pl.pallas_call(functools.partial(kernel, (nia, nja, nka, rank, ti, tj, tk...]
where the time goes in v3:
time: 79.9 us; the launch traced here: 79.7 us
  Pallas kernels  79.1 us (99%)
    pallas_call x1, Pallas kernels, on_device(): pl.pallas_call(functools.partial(kernel, (nia, nja, nka, rank, ti, tj, tk...  77.5 us
    pallas_call x1, Pallas kernels, on_device(): pl.pallas_call(hand_out, out_shape=shapes, in_specs=[in_vmem] * 3, out_sp...  1.65 us

profile of v3, /device:TPU:1, one launch (start us, length us, event | category | flops | bytes accessed | tf_op | source)
XLA Modules:
  0.0 79.7 jit_solution(9388650598975049674)
XLA Ops:
  0.6 77.5 %factor_round.1 = (bf16[256,256]{1,0:T(8,128)(2,1)}, bf16[128,256]{1,0:T(8,128)(2,1)}, bf16[128,256]{1,0:T(8,128)(2,1)}) custom-call(bf16[256,128,128]{2,1,0:T(8,128)(2,1)} %tensor_ref.1, bf16[2048,1024]{1,0:T(8,128)(2,1)} %matrix_ref.1, bf16[256,256]{1,0:T(8,128)(2,1)} %first_ref.1, bf16[128,256]{1,0:T(8,128)(2,1)} %second_ref.1, ...), custom_call_target="tpu_custom_call" | custom-call | tf_op jit(solution)/shard_map/factor_round/pallas_call | solution.py:592
  78.1 1.6 %hand_out.1 = (bf16[256,256]{1,0:T(8,128)(2,1)}, bf16[128,256]{1,0:T(8,128)(2,1)}, bf16[128,256]{1,0:T(8,128)(2,1)}) custom-call(bf16[256,256]{1,0:T(8,128)(2,1)} %get-tuple-element.6.first, bf16[128,256]{1,0:T(8,128)(2,1)} %get-tuple-element.7.second, bf16[128,256]{1,0:T(8,128)(2,1)} %get-tuple-element.8.time), custom_call_target="tpu_custom_call" | custom-call | tf_op jit(solution)/shard_map/hand_out/pallas_call | solution.py:603

commit v4 on v3

--- a/solution.py
+++ b/solution.py
@@ -383,25 +383,15 @@
     wait_bytes(fn_in.at[0, pl.ds(0, groups - 1)], recv_sem.at[7])
     fn_copy = remote(fn_in.at[core], fn_in.at[core], send_sem.at[12], recv_sem.at[12], ia, sibling, ka)
     fn_copy.start()
-    wait_bytes(gt_wide.at[pl.ds(0, nka - 1)], recv_sem.at[8])
-    gt_rows = jnp.sum(gt_wide[...], axis=0).reshape(q4, rank)
     fn_copy.wait_recv()
     fn_t = jnp.stack([fn_in[0].astype(F32), fn_in[1].astype(F32)], axis=1)
     fn_t = fn_t.reshape(rank, ti).astype(BF16)
     fn = transposed(fn_t).astype(BF16)
     first_out[...] = fn
-    gf_loc[...] = dot(fn_t, fn).reshape(nia, q4, rank)
-    gf_in[ia] = gf_loc[ia]
-
-    @pl.loop(0, nia - 1)
-    def _(t):
-        dia = ia_of(t)
-        remote(gf_loc.at[dia], gf_in.at[ia], send_sem.at[16], recv_sem.at[16], dia, ja, ka).start()
-
-    @pl.loop(0, half // 4)
+    @pl.loop(0, half // 8)
     def _(b):
-        for u in range(4):
-            j = b * 4 + u
+        for u in range(8):
+            j = b * 8 + u
             block = dot(turn[j], first_out[...])
             wide[j] = block
             sums = jnp.sum(block.reshape(2, tk, rank) * time_f[...][None], axis=1)
@@ -416,6 +406,16 @@
         dia = ia_of(t)
         remote(ps_loc.at[dia], ps_in.at[ia], send_sem.at[10], recv_sem.at[10], dia, ja, ka).start()
 
+    gf_loc[...] = dot(fn_t, first_out[...]).reshape(nia, q4, rank)
+    gf_in[ia] = gf_loc[ia]
+
+    @pl.loop(0, nia - 1)
+    def _(t):
+        dia = ia_of(t)
+        remote(gf_loc.at[dia], gf_in.at[ia], send_sem.at[16], recv_sem.at[16], dia, ja, ka).start()
+
+    wait_bytes(gt_wide.at[pl.ds(0, nka - 1)], recv_sem.at[8])
+    gt_rows = jnp.sum(gt_wide[...], axis=0).reshape(q4, rank)
     wait_bytes(ps_in.at[pl.ds(0, nia - 1)], recv_sem.at[10])
     pa_in[ka] = jnp.sum(ps_in[...], axis=0)
 

time: 79.9 us -> 78.1 us (0.977)
  Pallas kernels: 79.1 us -> 77.3 us
    pallas_call x1, Pallas kernels: 77.5 us -> 75.7 us  [on_device(): pl.pallas_call(functools.partial(kernel, (nia, nja, nka, rank, ti, tj, tk...]
where the time goes in v4:
time: 78.1 us; the launch traced here: 78 us
  Pallas kernels  77.3 us (99%)
    pallas_call x1, Pallas kernels, on_device(): pl.pallas_call(functools.partial(kernel, (nia, nja, nka, rank, ti, tj, tk...  75.7 us
    pallas_call x1, Pallas kernels, on_device(): pl.pallas_call(hand_out, out_shape=shapes, in_specs=[in_vmem] * 3, out_sp...  1.65 us

profile of v4, /device:TPU:1, one launch (start us, length us, event | category | flops | bytes accessed | tf_op | source)
XLA Modules:
  0.0 78.0 jit_solution(16119292022112395081)
XLA Ops:
  0.6 75.7 %factor_round.1 = (bf16[256,256]{1,0:T(8,128)(2,1)}, bf16[128,256]{1,0:T(8,128)(2,1)}, bf16[128,256]{1,0:T(8,128)(2,1)}) custom-call(bf16[256,128,128]{2,1,0:T(8,128)(2,1)} %tensor_ref.1, bf16[2048,1024]{1,0:T(8,128)(2,1)} %matrix_ref.1, bf16[256,256]{1,0:T(8,128)(2,1)} %first_ref.1, bf16[128,256]{1,0:T(8,128)(2,1)} %second_ref.1, ...), custom_call_target="tpu_custom_call" | custom-call | tf_op jit(solution)/shard_map/factor_round/pallas_call | solution.py:592
  76.3 1.6 %hand_out.1 = (bf16[256,256]{1,0:T(8,128)(2,1)}, bf16[128,256]{1,0:T(8,128)(2,1)}, bf16[128,256]{1,0:T(8,128)(2,1)}) custom-call(bf16[256,256]{1,0:T(8,128)(2,1)} %get-tuple-element.6.first, bf16[128,256]{1,0:T(8,128)(2,1)} %get-tuple-element.7.second, bf16[128,256]{1,0:T(8,128)(2,1)} %get-tuple-element.8.time), custom_call_target="tpu_custom_call" | custom-call | tf_op jit(solution)/shard_map/hand_out/pallas_call | solution.py:603

commit v5 on v4

--- a/solution.py
+++ b/solution.py
@@ -163,14 +163,6 @@
         rows = pl.ds(b * 16, 16)
         return pltpu.make_async_copy(tensor_ref.at[rows], tens.at[rows], tens_sem.at[b])
 
-    @pl.loop(0, nia)
-    def _(s):
-        mat_copy(s).start()
-
-    @pl.loop(0, ti // 16)
-    def _(b):
-        tens_copy(b).start()
-
     barrier = pltpu.get_barrier_semaphore()
 
     def greet(dia, dja, dka):
@@ -190,6 +182,14 @@
 
     greet(ia, 2 * (1 - yh) + other, ka)
     greet(ia, sibling, ka)
+    @pl.loop(0, nia)
+    def _(s):
+        mat_copy(s).start()
+
+    @pl.loop(0, ti // 16)
+    def _(b):
+        tens_copy(b).start()
+
     col_t[...] = transposed(column_ref[...]).astype(BF16)
 
     def pair_copy(s):
@@ -447,17 +447,16 @@
         remote(gn_loc.at[dja], gn_in.at[ja], send_sem.at[13], recv_sem.at[13], ia, dja, ka).start()
 
     sn_rows = transposed(sn_t)
-    second_out[...] = sn_rows.astype(BF16)
     sn_f[...] = sn_rows
 
     def add_planes(b, total):
-        for u in range(4):
-            j = b * 4 + u
+        for u in range(8):
+            j = b * 8 + u
             total = total + wide[j, :tk] * sn_f[pl.ds(j, 1), :]
             total = total + wide[j, tk:] * sn_f[pl.ds(j + half, 1), :]
         return total
 
-    tsum = lax.fori_loop(0, half // 4, add_planes, jnp.zeros((tk, rank), F32))
+    tsum = lax.fori_loop(0, half // 8, add_planes, jnp.zeros((tk, rank), F32))
     ts_loc[...] = tsum.T.reshape(nia * nja, q3, tk)
     ts_in[slot3] = ts_loc[slot3]
 
@@ -468,6 +467,7 @@
             ts_loc.at[dia * nja + dja], ts_in.at[slot3], send_sem.at[14], recv_sem.at[14], dia, dja, ka
         ).start()
 
+    second_out[...] = sn_f[...].astype(BF16)
     wait_bytes(gn_in.at[pl.ds(0, nja - 1)], recv_sem.at[13])
     gram_rows = gf_sum[ja] * jnp.sum(gn_in[...], axis=0)
     time_den = exact_product(gram_rows, time_ref[...])

time: 78.1 us -> 77.8 us (level)
  no operation moved by 1% of the time
where the time goes in v5:
time: 77.8 us; the launch traced here: 77.7 us
  Pallas kernels  77 us (99%)
    pallas_call x1, Pallas kernels, on_device(): pl.pallas_call(functools.partial(kernel, (nia, nja, nka, rank, ti, tj, tk...  75.4 us
    pallas_call x1, Pallas kernels, on_device(): pl.pallas_call(hand_out, out_shape=shapes, in_specs=[in_vmem] * 3, out_sp...  1.65 us

profile of v5, /device:TPU:1, one launch (start us, length us, event | category | flops | bytes accessed | tf_op | source)
XLA Modules:
  0.0 77.7 jit_solution(13095412108279438637)
XLA Ops:
  0.6 75.4 %factor_round.1 = (bf16[256,256]{1,0:T(8,128)(2,1)}, bf16[128,256]{1,0:T(8,128)(2,1)}, bf16[128,256]{1,0:T(8,128)(2,1)}) custom-call(bf16[256,128,128]{2,1,0:T(8,128)(2,1)} %tensor_ref.1, bf16[2048,1024]{1,0:T(8,128)(2,1)} %matrix_ref.1, bf16[256,256]{1,0:T(8,128)(2,1)} %first_ref.1, bf16[128,256]{1,0:T(8,128)(2,1)} %second_ref.1, ...), custom_call_target="tpu_custom_call" | custom-call | tf_op jit(solution)/shard_map/factor_round/pallas_call | solution.py:592
  76.0 1.6 %hand_out.1 = (bf16[256,256]{1,0:T(8,128)(2,1)}, bf16[128,256]{1,0:T(8,128)(2,1)}, bf16[128,256]{1,0:T(8,128)(2,1)}) custom-call(bf16[256,256]{1,0:T(8,128)(2,1)} %get-tuple-element.6.first, bf16[128,256]{1,0:T(8,128)(2,1)} %get-tuple-element.7.second, bf16[128,256]{1,0:T(8,128)(2,1)} %get-tuple-element.8.time), custom_call_target="tpu_custom_call" | custom-call | tf_op jit(solution)/shard_map/hand_out/pallas_call | solution.py:603
